TPU v7x, 256 devices: a whole 4x4x8 slice. The times are simulated.
256 devices in a mesh: grp: 4 (over y), shard: 64 (over z, x, core).
Axes of the slice: x: 4, y: 4, z: 8, core: 2. Of those that a mesh axis runs over, the one named last changes fastest.
Arguments:
- query_rows: bfloat16 [65536, 1024], P(('grp', 'shard')), may hold values from -6 to 6
- key_rows: bfloat16 [65536, 1024], P(('grp', 'shard')), may hold values from -6 to 6
- value_rows: bfloat16 [65536, 1024], P(('grp', 'shard')), may hold values from -6 to 6
- grad_out: bfloat16 [65536, 1024], P(('grp', 'shard')), may hold values from -6 to 6
Outputs:
- attended: bfloat16 [65536, 1024], P(('grp', 'shard'))
- grad_query: bfloat16 [65536, 1024], P(('grp', 'shard'))
- grad_key: bfloat16 [65536, 1024], P(('grp', 'shard'))
- grad_value: bfloat16 [65536, 1024], P(('grp', 'shard'))
All inputs are finite; a program needn't handle non-finite values.
Results may differ from a plain program's by a relative error of at most 0.012.
Values may be sent and summed in bfloat16 or wider, within the bound.
A program may use at most 256 MiB of HBM per device.

v0:
```python
import jax
import jax.numpy as jnp
from jax import lax
from jax.sharding import PartitionSpec as P

HD = 128


def entering(array, axis, join, neutral, backward):
    count = lax.axis_size(axis)
    place = lax.axis_index(axis)
    ahead = count - 1 - place if backward else place
    gathered = lax.all_gather(array.astype(jnp.bfloat16), axis)
    state = jnp.zeros_like(array) + jnp.asarray(neutral, array.dtype)

    def one(step, state):
        source = count - 1 - step if backward else step
        return join(state, lax.dynamic_index_in_dim(gathered, source, 0, False).astype(array.dtype))

    return lax.fori_loop(0, ahead, one, state)


def add_states(earlier, later_part):
    return earlier + later_part


def prefix_states(local_state, backward):
    empty_state = jnp.zeros_like(local_state)
    inside = entering(local_state, "shard", add_states, empty_state, backward)
    group_sum = lax.psum(local_state, "shard")
    outside = entering(group_sum, "grp", add_states, empty_state, backward)
    return inside + outside


def body(query_rows, key_rows, value_rows, grad_out):
    row_count = query_rows.shape[0]
    head_size = HD
    head_count = query_rows.shape[1] // head_size
    query_heads = query_rows.reshape(row_count, head_count, head_size)
    key_heads = key_rows.reshape(row_count, head_count, head_size)
    value_heads = value_rows.reshape(row_count, head_count, head_size)
    rows_at = lax.broadcasted_iota(jnp.int32, (row_count, row_count), 0)
    cols_at = lax.broadcasted_iota(jnp.int32, (row_count, row_count), 1)
    causal = (rows_at >= cols_at)[None]
    block_state = jnp.einsum(
        "thd,the->hde", key_heads, value_heads, preferred_element_type=jnp.float32
    )
    earlier = prefix_states(block_state, False)
    scores = jnp.einsum("thd,shd->hts", query_heads, key_heads, preferred_element_type=jnp.float32)
    local_scores = jnp.where(causal, scores, 0.0).astype(jnp.bfloat16)
    local_mixed = jnp.einsum(
        "hts,she->the", local_scores, value_heads, preferred_element_type=jnp.float32
    )
    earlier_rounded = earlier.astype(jnp.bfloat16)
    mixed_rows = local_mixed + jnp.einsum(
        "thd,hde->the", query_heads, earlier_rounded, preferred_element_type=jnp.float32
    )
    inv_rms = lax.rsqrt(jnp.mean(mixed_rows * mixed_rows, axis=-1, keepdims=True) + 1.0)
    normed = mixed_rows * inv_rms
    attended = normed.astype(jnp.bfloat16).reshape(row_count, head_count * head_size)
    grad_heads = grad_out.reshape(row_count, head_count, head_size).astype(jnp.float32)
    grad_mixed = (
        (grad_heads - normed * jnp.mean(grad_heads * normed, axis=-1, keepdims=True)) * inv_rms
    ).astype(jnp.bfloat16)
    block_reverse = jnp.einsum(
        "thd,the->hde", query_heads, grad_mixed, preferred_element_type=jnp.float32
    )
    later_sum = prefix_states(block_reverse, True)
    grad_raw = jnp.einsum(
        "the,she->hts", grad_mixed, value_heads, preferred_element_type=jnp.float32
    )
    grad_scores = jnp.where(causal, grad_raw, 0.0).astype(jnp.bfloat16)
    grad_query = jnp.einsum(
        "hts,shd->thd", grad_scores, key_heads, preferred_element_type=jnp.float32
    )
    grad_query = grad_query + jnp.einsum(
        "the,hde->thd", grad_mixed, earlier_rounded, preferred_element_type=jnp.float32
    )
    key_local = jnp.einsum(
        "hts,thd->shd", grad_scores, query_heads, preferred_element_type=jnp.float32
    )
    value_local = jnp.einsum(
        "hts,the->she", local_scores, grad_mixed, preferred_element_type=jnp.float32
    )
    later_rounded = later_sum.astype(jnp.bfloat16)
    grad_key = key_local + jnp.einsum(
        "she,hde->shd", value_heads, later_rounded, preferred_element_type=jnp.float32
    )
    grad_value = value_local + jnp.einsum(
        "shd,hde->she", key_heads, later_rounded, preferred_element_type=jnp.float32
    )
    flat_width = head_count * head_size
    return (
        attended,
        grad_query.astype(jnp.bfloat16).reshape(row_count, flat_width),
        grad_key.astype(jnp.bfloat16).reshape(row_count, flat_width),
        grad_value.astype(jnp.bfloat16).reshape(row_count, flat_width),
    )


def solution(mesh):
    in_specs = (
        P(("grp", "shard"), None),
        P(("grp", "shard"), None),
        P(("grp", "shard"), None),
        P(("grp", "shard"), None),
    )
    out_specs = (
        P(("grp", "shard"), None),
        P(("grp", "shard"), None),
        P(("grp", "shard"), None),
        P(("grp", "shard"), None),
    )
    return jax.shard_map(body, mesh=mesh, in_specs=in_specs, out_specs=out_specs, check_vma=False)
```

profile of v0, /device:TPU:1, one launch (start us, length us, event | category | flops | bytes accessed | tf_op | source)
XLA Modules:
  0.0 917.8 jit_solution(16972495328482349829)
XLA Ops:
  7.2 1.2 copy.61
  9.8 252.9 %all-reduce.2 = bf16[8,128,128]{2,1,0:T(8,128)(2,1)} all-reduce(f32[8,128,128]{2,1,0:T(8,128)S(1)} %get-tuple-element.217), channel_id=1, replica_groups=mesh['grp'=4,'shard'=64] {'shard'}, use_global_device_ids=true, to_apply=%region_2.3 | all-reduce | flops 131072 | bytes 786432 | tf_op jit(solution)/shard_map/psum | solution.py:30
  263.5 1.2 copy.38
  266.3 1.5 convolution_bitcast_fusion.5
  267.7 19.5 %all-gather.11.cloned.1.call-done = bf16[32,128,128]{2,1,0:T(8,128)(2,1)} async-done(((bf16[8,128,128]{2,1,0:T(8,128)(2,1)}), bf16[32,128,128]{2,1,0:T(8,128)(2,1)}) %all-gather.11.cloned.1.call-update) | async-done | bytes 1048592 | tf_op jit(solution)/shard_map/all_gather | solution.py:13
  287.3 105.4 %all-gather.9.cloned.1.call-done = bf16[512,128,128]{2,1,0:T(8,128)(2,1)} async-done(((bf16[8,128,128]{2,1,0:T(8,128)(2,1)}), bf16[512,128,128]{2,1,0:T(8,128)(2,1)}) %all-gather.9.cloned.1.call-update) | async-done | bytes 16777232 | tf_op jit(solution)/shard_map/all_gather | solution.py:13
  392.7 1.1 while.44
  393.9 1.6 multiply_reduce_fusion.1
  397.0 313.1 %all-reduce.3 = bf16[8,128,128]{1,2,0:T(8,128)(2,1)S(1)} all-reduce(f32[8,128,128]{1,2,0:T(8,128)S(1)} %get-tuple-element.221), channel_id=1, replica_groups=mesh['grp'=4,'shard'=64] {'shard'}, use_global_device_ids=true, to_apply=%region_9.10 | all-reduce | flops 131072 | bytes 786432 | tf_op jit(solution)/shard_map/psum | solution.py:30
  712.9 1.1 fusion.3
  714.0 2.0 copy.51
  717.0 1.3 fusion.29
  718.7 15.7 %all-gather.15.cloned.1.call-done = bf16[32,128,128]{2,1,0:T(8,128)(2,1)} async-done(((bf16[8,128,128]{2,1,0:T(8,128)(2,1)}), bf16[32,128,128]{2,1,0:T(8,128)(2,1)}) %all-gather.15.cloned.1.call-update) | async-done | bytes 1048592 | tf_op jit(solution)/shard_map/all_gather | solution.py:13
  734.4 3.3 while.47
  734.4 1.1 convert_add_fusion.11
  735.5 1.1 convert_add_fusion.11
  736.6 1.1 convert_add_fusion.11
  737.7 101.4 %all-gather.13.cloned.1.call-done = bf16[512,128,128]{2,1,0:T(8,128)(2,1)} async-done(((bf16[8,128,128]{2,1,0:T(8,128)(2,1)}), bf16[512,128,128]{2,1,0:T(8,128)(2,1)}) %all-gather.13.cloned.1.call-update) | async-done | bytes 16777232 | tf_op jit(solution)/shard_map/all_gather | solution.py:13
  839.1 68.0 %while.46 = (s32[]{:T(128)}, f32[8,128,128]{2,1,0:T(8,128)S(1)}, s32[]{:T(128)}, bf16[64,8,128,128]{3,2,1,0:T(8,128)(2,1)}, s32[]{:T(128)}, /*index=5*/s32[]{:T(128)}, s32[]{:T(128)}, s32[]{:T(128)}) while((s32[]{:T(128)}, f32[8,128,128]{2,1,0:T(8,128)S(1)}, s32[]{:T(128)}, bf16[64,8,128,128]{3,2,1,0:T(8,128)(2,1)}, s32[]{:T(128)}, ...), condition=%wide.region_8.9_spmd, body=%wide.region_7.8_spmd.sunk | while | flops 262150 | bytes 1310855 | solution.py:20
  840.2 1.1 convert_add_fusion.10
  841.3 1.1 convert_add_fusion.10
  842.4 1.1 convert_add_fusion.10
  843.5 1.1 convert_add_fusion.10
  844.6 1.1 convert_add_fusion.10
  845.7 1.1 convert_add_fusion.10
  846.8 1.1 convert_add_fusion.10
  851.2 1.1 convert_add_fusion.10
  852.3 1.1 convert_add_fusion.10
  853.4 1.1 convert_add_fusion.10
  854.5 1.1 convert_add_fusion.10
  855.6 1.1 convert_add_fusion.10
  856.7 1.1 convert_add_fusion.10
  861.1 1.1 convert_add_fusion.10
  862.2 1.1 convert_add_fusion.10
  863.3 1.1 convert_add_fusion.10
  864.4 1.1 convert_add_fusion.10
  865.5 1.1 convert_add_fusion.10
  866.6 1.1 convert_add_fusion.10
  867.6 1.1 convert_add_fusion.10
  872.0 1.1 convert_add_fusion.10
  873.1 1.1 convert_add_fusion.10
  874.2 1.1 convert_add_fusion.10
  875.3 1.1 convert_add_fusion.10
  876.4 1.1 convert_add_fusion.10
  877.5 1.1 convert_add_fusion.10
  881.9 1.1 convert_add_fusion.10
  883.0 1.1 convert_add_fusion.10
  907.2 1.7 fusion.5
  (90 shorter events, 49.2 us)
Async XLA Ops:
  7.2 257.7 %copy-start = (bf16[256,1024]{1,0:T(8,128)(2,1)S(1)}, bf16[256,1024]{1,0:T(8,128)(2,1)}, u32[]{:S(2)}) copy-start(bf16[256,1024]{1,0:T(8,128)(2,1)} %param.12) | copy-start | bytes 1572868
  7.2 1.6 copy-start.3
  7.2 280.0 %all-gather.11.cloned.1.call-start = ((), (), s32[]{:S(2)}) async-start(), calls=%async_computation.1 | async-start | bytes 1310720 | tf_op jit(solution)/shard_map/all_gather | solution.py:13
  8.8 256.0 %copy-start.1 = (bf16[256,8,128]{0,2,1:T(8,128)(2,1)}, bf16[256,8,128]{0,2,1:T(8,128)(2,1)S(1)}, u32[]{:S(2)}) copy-start(bf16[256,8,128]{0,2,1:T(8,128)(2,1)S(1)} %copy.34) | copy-start | bytes 1572868
  8.8 256.0 %copy-start.9 = (bf16[256,1024]{1,0:T(8,128)(2,1)S(1)}, bf16[256,1024]{1,0:T(8,128)(2,1)}, u32[]{:S(2)}) copy-start(bf16[256,1024]{1,0:T(8,128)(2,1)} %param.13) | copy-start | bytes 1572868
  262.7 129.9 %all-gather.9.cloned.1.call-start = ((), (), s32[]{:S(2)}) async-start(), calls=%async_computation | async-start | bytes 17039360 | tf_op jit(solution)/shard_map/all_gather | solution.py:13
  263.5 470.9 %all-gather.15.cloned.1.call-start = ((), (), s32[]{:S(2)}) async-start(), calls=%async_computation.3 | async-start | bytes 1310720 | tf_op jit(solution)/shard_map/all_gather | solution.py:13
  265.3 1.0 copy-start.5
  396.7 315.2 %copy-start.4 = (bf16[256,1024]{1,0:T(8,128)(2,1)S(1)}, bf16[256,1024]{1,0:T(8,128)(2,1)}, u32[]{:S(2)}) copy-start(bf16[256,1024]{1,0:T(8,128)(2,1)} %param.14) | copy-start | bytes 1572868
  710.0 2.3 copy-start.2
  710.9 128.1 %all-gather.13.cloned.1.call-start = ((), (), s32[]{:S(2)}) async-start(), calls=%async_computation.2 | async-start | bytes 17039360 | tf_op jit(solution)/shard_map/all_gather | solution.py:13
  712.4 1.6 copy-start.7
  712.9 3.1 copy-start.10
  712.9 4.1 copy-start.6
  717.0 1.3 copy-start.8
Sparse Core Ops, SparseCore 0:
  262.9 24.3 all-gather.10
  290.6 102.0 all-gather.8
  711.0 23.2 all-gather.14
  737.0 102.0 all-gather.12
where the time goes:
time: 920 us; the launch traced here: 918 us
  blocking collectives  566 us (62%)
  waiting for transfers between devices  243 us (26%)
  other arithmetic  71.9 us (8%)
  between operations  14 us (2%)
  local copies, waits for them, and re-layouts  10.7 us (1%)
  matrix products  10.5 us (1%)
    psum x2, blocking collectives, prefix_states(): group_sum = lax.psum(local_state, 'shard')  566 us
    all_gather x4, waiting for transfers between devices, entering(): gathered = lax.all_gather(array.astype(jnp.bfloat16), axis)  242 us
    add x66, other arithmetic, add_states(): return earlier + later_part  70.6 us
  transfers between devices with their start and end apart: 4, of which 4 were waited for; matrix products, arithmetic and copies ran while one was open for 2% of the time, Pallas kernels for 0%

commit v1 on v0

--- a/solution.py
+++ b/solution.py
@@ -27,7 +27,7 @@
 def prefix_states(local_state, backward):
     empty_state = jnp.zeros_like(local_state)
     inside = entering(local_state, "shard", add_states, empty_state, backward)
-    group_sum = lax.psum(local_state, "shard")
+    group_sum = jnp.sum(lax.all_gather(local_state, "shard"), axis=0)
     outside = entering(group_sum, "grp", add_states, empty_state, backward)
     return inside + outside
 

time: 920 us -> 653 us (0.71)
  blocking collectives: 566 us -> 0 us
  waiting for transfers between devices: 243 us -> 513 us
  other arithmetic: 71.9 us -> 96.4 us
    psum x2 -> x0, blocking collectives: 566 us -> none  [prefix_states(): group_sum = lax.psum(local_state, 'shard')]
    all_gather x0 -> x2, waiting for transfers between devices: none -> 322 us  [prefix_states(): group_sum = jnp.sum(lax.all_gather(local_state, 'shard'), axis=0)]
    all_gather x4, waiting for transfers between devices: 242 us -> 190 us  [entering(): gathered = lax.all_gather(array.astype(jnp.bfloat16), axis)]
    reduce_sum x0 -> x2, other arithmetic: none -> 24.4 us  [prefix_states(): group_sum = jnp.sum(lax.all_gather(local_state, 'shard'), axis=0)]
  transfers between devices with their start and end apart: 4 -> 6, of which waited for: 4 -> 5; matrix products, arithmetic and copies ran while one was open for 2% -> 16% of each run, Pallas kernels for 0% -> 0%
where the time goes in v1:
time: 653 us; the launch traced here: 651 us
  waiting for transfers between devices  513 us (79%)
  other arithmetic  96.4 us (15%)
  between operations  14.4 us (2%)
  matrix products  13.2 us (2%)
  local copies, waits for them, and re-layouts  12.3 us (2%)
    all_gather x2, waiting for transfers between devices, prefix_states(): group_sum = jnp.sum(lax.all_gather(local_state, 'shard'), axis=0)  322 us
    all_gather x4, waiting for transfers between devices, entering(): gathered = lax.all_gather(array.astype(jnp.bfloat16), axis)  190 us
    add x66, other arithmetic, add_states(): return earlier + later_part  70.6 us
    reduce_sum x2, other arithmetic, prefix_states(): group_sum = jnp.sum(lax.all_gather(local_state, 'shard'), axis=0)  24.4 us
  transfers between devices with their start and end apart: 6, of which 5 were waited for; matrix products, arithmetic and copies ran while one was open for 16% of the time, Pallas kernels for 0%

profile of v1, /device:TPU:1, one launch (start us, length us, event | category | flops | bytes accessed | tf_op | source)
XLA Modules:
  0.0 650.9 jit_solution(13207112905633814764)
XLA Ops:
  7.2 1.2 copy.63
  8.7 2.2 fusion.27
  11.8 1.2 copy.37
  13.1 144.1 %all-gather.15.cloned.1.call-done = f32[512,128,128]{2,1,0:T(8,128)} async-done(((f32[8,128,128]{2,1,0:T(8,128)}), f32[512,128,128]{2,1,0:T(8,128)}) %all-gather.15.cloned.1.call-update) | async-done | bytes 33554448 | tf_op jit(solution)/shard_map/all_gather | solution.py:30
  157.1 12.6 %reduce_sum.36 = bf16[8,128,128]{2,1,0:T(8,128)(2,1)} reduce(f32[64,8,128,128]{3,2,1,0:T(8,128)} %bitcast.138, f32[]{:T(128)} %constant.79.clone.1), dimensions={0}, to_apply=%region_2.3 | reduce | flops 8257536 | bytes 33816580 | tf_op jit(solution)/shard_map/reduce_sum | solution.py:30
  171.3 1.5 convolution_bitcast_fusion.5
  172.8 83.9 %all-gather.13.cloned.1.call-done = bf16[512,128,128]{2,1,0:T(8,128)(2,1)} async-done(((bf16[8,128,128]{2,1,0:T(8,128)(2,1)}), bf16[512,128,128]{2,1,0:T(8,128)(2,1)}) %all-gather.13.cloned.1.call-update) | async-done | bytes 16777232 | tf_op jit(solution)/shard_map/all_gather | solution.py:13
  256.8 1.1 while.44
  256.8 1.1 convert_add_fusion.8
  257.9 22.5 %all-gather.17.cloned.1.call-done = bf16[32,128,128]{2,1,0:T(8,128)(2,1)} async-done(((bf16[8,128,128]{2,1,0:T(8,128)(2,1)}), bf16[32,128,128]{2,1,0:T(8,128)(2,1)}) %all-gather.17.cloned.1.call-update) | async-done | bytes 1048592 | tf_op jit(solution)/shard_map/all_gather | solution.py:13
  280.5 1.6 multiply_reduce_fusion.1
  285.6 1.5 select_convert_fusion
  289.4 2.0 copy.51
  291.4 178.2 %all-gather.21.cloned.1.call-done = f32[512,128,128]{2,1,0:T(8,128)} async-done(((f32[8,128,128]{2,1,0:T(8,128)}), f32[512,128,128]{2,1,0:T(8,128)}) %all-gather.21.cloned.1.call-update) | async-done | bytes 33554448 | tf_op jit(solution)/shard_map/all_gather | solution.py:30
  469.6 11.8 %reduce_sum.39 = bf16[8,128,128]{2,1,0:T(8,128)(2,1)S(1)} reduce(f32[64,8,128,128]{3,2,1,0:T(8,128)} %bitcast.137, f32[]{:T(128)} %constant.79.clone.1), dimensions={0}, to_apply=%region_9.10 | reduce | flops 8257536 | bytes 33816580 | tf_op jit(solution)/shard_map/reduce_sum | solution.py:30
  482.5 1.3 fusion.29
  483.8 1.6 convolution_bitcast_fusion.3
  485.3 83.1 %all-gather.19.cloned.1.call-done = bf16[512,128,128]{2,1,0:T(8,128)(2,1)} async-done(((bf16[8,128,128]{2,1,0:T(8,128)(2,1)}), bf16[512,128,128]{2,1,0:T(8,128)(2,1)}) %all-gather.19.cloned.1.call-update) | async-done | bytes 16777232 | tf_op jit(solution)/shard_map/all_gather | solution.py:13
  568.5 68.0 %while.46 = (s32[]{:T(128)}, f32[8,128,128]{2,1,0:T(8,128)S(1)}, s32[]{:T(128)}, bf16[64,8,128,128]{3,2,1,0:T(8,128)(2,1)}, s32[]{:T(128)}, /*index=5*/s32[]{:T(128)}, s32[]{:T(128)}, s32[]{:T(128)}) while((s32[]{:T(128)}, f32[8,128,128]{2,1,0:T(8,128)S(1)}, s32[]{:T(128)}, bf16[64,8,128,128]{3,2,1,0:T(8,128)(2,1)}, s32[]{:T(128)}, ...), condition=%wide.region_8.9_spmd, body=%wide.region_7.8_spmd.sunk | while | flops 262150 | bytes 1310855 | solution.py:20
  571.8 1.1 convert_add_fusion.10
  572.9 1.1 convert_add_fusion.10
  574.0 1.1 convert_add_fusion.10
  575.1 1.1 convert_add_fusion.10
  576.2 1.1 convert_add_fusion.10
  577.3 1.1 convert_add_fusion.10
  578.4 1.1 convert_add_fusion.10
  579.5 1.1 convert_add_fusion.10
  580.6 1.1 convert_add_fusion.10
  583.9 1.1 convert_add_fusion.10
  585.0 1.1 convert_add_fusion.10
  586.1 1.1 convert_add_fusion.10
  587.2 1.1 convert_add_fusion.10
  588.3 1.1 convert_add_fusion.10
  589.4 1.1 convert_add_fusion.10
  593.8 1.1 convert_add_fusion.10
  594.9 1.1 convert_add_fusion.10
  595.9 1.1 convert_add_fusion.10
  597.0 1.1 convert_add_fusion.10
  598.1 1.1 convert_add_fusion.10
  599.2 1.1 convert_add_fusion.10
  603.6 1.1 convert_add_fusion.10
  604.7 1.1 convert_add_fusion.10
  605.8 1.1 convert_add_fusion.10
  606.9 1.1 convert_add_fusion.10
  608.0 1.1 convert_add_fusion.10
  609.1 1.1 convert_add_fusion.10
  636.6 3.3 while.47
  640.0 1.7 fusion.5
  (90 shorter events, 52.7 us)
Async XLA Ops:
  7.2 162.7 %copy-start = (bf16[256,1024]{1,0:T(8,128)(2,1)S(1)}, bf16[256,1024]{1,0:T(8,128)(2,1)}, u32[]{:S(2)}) copy-start(bf16[256,1024]{1,0:T(8,128)(2,1)} %param.12) | copy-start | bytes 1572868
  7.2 150.0 %all-gather.15.cloned.1.call-start = ((), (), s32[]{:S(2)}) async-start(), calls=%async_computation.1 | async-start | bytes 34078720 | tf_op jit(solution)/shard_map/all_gather | solution.py:30
  11.0 245.7 %all-gather.13.cloned.1.call-start = ((), (), s32[]{:S(2)}) async-start(), calls=%async_computation | async-start | bytes 17039360 | tf_op jit(solution)/shard_map/all_gather | solution.py:13
  11.7 268.6 %all-gather.17.cloned.1.call-start = ((), (), s32[]{:S(2)}) async-start(), calls=%async_computation.2 | async-start | bytes 1310720 | tf_op jit(solution)/shard_map/all_gather | solution.py:13
  157.1 12.7 %copy-start.6 = (bf16[256,1024]{1,0:T(8,128)(2,1)S(1)}, bf16[256,1024]{1,0:T(8,128)(2,1)}, u32[]{:S(2)}) copy-start(bf16[256,1024]{1,0:T(8,128)(2,1)} %param.13) | copy-start | bytes 1572868
  157.1 14.2 %copy-start.1 = (bf16[256,1024]{1,0:T(8,128)(2,1)S(1)}, bf16[256,1024]{1,0:T(8,128)(2,1)}, u32[]{:S(2)}) copy-start(bf16[256,1024]{1,0:T(8,128)(2,1)} %param.14) | copy-start | bytes 1572868
  169.8 299.8 %all-gather.21.cloned.1.call-start = ((), (), s32[]{:S(2)}) async-start(), calls=%async_computation.4 | async-start | bytes 34078720 | tf_op jit(solution)/shard_map/all_gather | solution.py:30
  170.3 1.0 copy-start.3
  284.6 283.8 %all-gather.19.cloned.1.call-start = ((), (), s32[]{:S(2)}) async-start(), calls=%async_computation.3 | async-start | bytes 17039360 | tf_op jit(solution)/shard_map/all_gather | solution.py:13
  285.5 351.0 %all-gather.23.cloned.1.call-start = ((), (), s32[]{:S(2)}) async-start(), calls=%async_computation.5 | async-start | bytes 1310720 | tf_op jit(solution)/shard_map/all_gather | solution.py:13
  287.1 1.0 copy-start.5
  469.6 12.9 %copy-start.4 = (bf16[8,256,256]{2,1,0:T(8,128)(2,1)S(1)}, bf16[8,256,256]{2,1,0:T(8,128)(2,1)}, u32[]{:S(2)}) copy-start(bf16[8,256,256]{2,1,0:T(8,128)(2,1)} %copy-done.3) | copy-start | bytes 3145732
  481.4 161.3 %copy-start.2 = (bf16[256,1024]{1,0:T(8,128)(2,1)S(1)}, bf16[256,1024]{1,0:T(8,128)(2,1)}, u32[]{:S(2)}) copy-start(bf16[256,1024]{1,0:T(8,128)(2,1)} %param.14) | copy-start | bytes 1572868
Sparse Core Ops, SparseCore 0:
  11.3 145.7 all-gather.14
  160.5 96.1 all-gather.12
  259.1 21.2 all-gather.16
  284.7 184.8 all-gather.20
  472.2 96.1 all-gather.18
  570.7 21.2 all-gather.22
